TPU v7x, 32 devices: a whole 2x2x4 slice. The times are simulated.
32 devices in a mesh: grp: 2 (over y), row: 8 (over z, core), col: 2 (over x).
Axes of the slice: x: 2, y: 2, z: 4, core: 2. Of those that a mesh axis runs over, the one named last changes fastest.
Arguments:
- pair: bfloat16 [192, 96, 128], P(('grp', 'row'), 'col'), parts along dimension 0, may hold values from -6 to 6
- token_count: int32 [2], P('grp'), parts along dimension 0, may hold values from 72 to 96
- tri_in: bfloat16 [2, 128, 512], replicated, may hold values from -0.5 to 0.5
- tri_gate: bfloat16 [2, 128, 128], replicated, may hold values from -0.5 to 0.5
- tri_out: bfloat16 [2, 128, 128], replicated, may hold values from -0.5 to 0.5
- trans_in: bfloat16 [128, 1024], replicated, may hold values from -0.5 to 0.5
- trans_out: bfloat16 [512, 128], replicated, may hold values from -0.25 to 0.25
Outputs:
- pair_out: bfloat16 [192, 96, 128], P(('grp', 'row'), 'col'), parts along dimension 0
There are 2 independent parts, one for each index of `grp`. A program takes and returns all parts, laid end to end along the dimension named above; an argument that names none is the same for every part. Nothing has to cross between parts.
Inputs may be any that keep to these rules, and one draw needn't show every extreme that they name: `token_count`: the number of real tokens of the complex; pair entries with either token index at or past it are padding.
All inputs are finite; a program needn't handle non-finite values.
Results may differ from a plain program's by a relative error of at most 0.015.
Values may be sent and summed in bfloat16 or wider, within the bound.
No kernel may reach another device: no remote copies, remote signals or barrier semaphores. Data moves between devices by JAX's collectives and lax.ppermute only.
A program may use at most 64 MiB of HBM per device.

v0:
```python
import jax
import jax.numpy as jnp
from jax import lax
from jax.sharding import PartitionSpec as P


def layer_norm(values, along):
    average = jnp.mean(values, axis=along, keepdims=True)
    centred = values - average
    spread = jnp.mean(centred * centred, axis=along, keepdims=True)
    return centred * lax.rsqrt(spread + 1e-05)


def contract_rows(left_side, right_side):
    return jnp.einsum("hik,hjk->hij", left_side, right_side, preferred_element_type=jnp.float32)


def contract_columns(left_side, right_side):
    return jnp.einsum("hki,hkj->hij", left_side, right_side, preferred_element_type=jnp.float32)


def body(pair, token_count, tri_in, tri_gate, tri_out, trans_in, trans_out):
    tile_rows, tile_cols, pair_width = pair.shape
    hidden = tri_out.shape[1]
    ffn_width = trans_out.shape[0]
    row_place = lax.axis_index("row")
    col_place = lax.axis_index("col")
    row_first = row_place * tile_rows
    col_first = col_place * tile_cols
    token_limit = token_count[0]
    row_keep = (row_first + jnp.arange(tile_rows, dtype=jnp.int32) < token_limit).astype(
        jnp.float32
    )
    col_keep = (col_first + jnp.arange(tile_cols, dtype=jnp.int32) < token_limit).astype(
        jnp.float32
    )
    keep_mask = row_keep[:, None] * col_keep[None, :]

    def project(stream, which_side):
        normed = layer_norm(stream.astype(jnp.float32), 2).astype(jnp.bfloat16)
        weight = tri_in[which_side].reshape(pair_width, 4, hidden)
        projected = jnp.einsum("ijc,cgh->ghij", normed, weight, preferred_element_type=jnp.float32)
        left_side = (keep_mask * jax.nn.sigmoid(projected[2]) * projected[0]).astype(jnp.bfloat16)
        right_side = (keep_mask * jax.nn.sigmoid(projected[3]) * projected[1]).astype(jnp.bfloat16)
        gate_value = jax.nn.sigmoid(
            jnp.dot(normed, tri_gate[which_side], preferred_element_type=jnp.float32)
        )
        return (left_side, right_side, gate_value)

    def finish(stream, mixed_sum, gate_value, which_side):
        normed = layer_norm(mixed_sum, 0).astype(jnp.bfloat16)
        update = gate_value * jnp.einsum(
            "hij,hc->ijc", normed, tri_out[which_side], preferred_element_type=jnp.float32
        )
        return (stream.astype(jnp.float32) + keep_mask[:, :, None] * update).astype(jnp.bfloat16)

    left_side, right_side, gate_value = project(pair, 0)
    partial_rows = contract_rows(left_side, lax.all_gather(right_side, "row", axis=1, tiled=True))
    mixed_sum = lax.psum_scatter(partial_rows, "col", scatter_dimension=2, tiled=True)
    stream = finish(pair, mixed_sum, gate_value, 0)
    left_side, right_side, gate_value = project(stream, 1)
    left_rows = lax.all_gather(left_side, "col", axis=2, tiled=True)
    column_strip = lax.all_to_all(left_rows, "row", split_axis=2, concat_axis=1, tiled=True)
    mixed_sum = contract_columns(
        column_strip, lax.all_gather(right_side, "row", axis=1, tiled=True)
    )
    stream = finish(stream, mixed_sum, gate_value, 1)
    normed = layer_norm(stream.astype(jnp.float32), 2).astype(jnp.bfloat16)
    inner_sum = jnp.dot(normed, trans_in, preferred_element_type=jnp.float32)
    activation = (jax.nn.silu(inner_sum[..., :ffn_width]) * inner_sum[..., ffn_width:]).astype(
        jnp.bfloat16
    )
    update = jnp.dot(activation, trans_out, preferred_element_type=jnp.float32)
    return (stream.astype(jnp.float32) + keep_mask[:, :, None] * update).astype(jnp.bfloat16)


def solution(mesh):
    placed = (P(("grp", "row"), "col", None), P("grp"), P(), P(), P(), P(), P())
    return jax.shard_map(
        body, mesh=mesh, in_specs=placed, out_specs=P(("grp", "row"), "col", None), check_vma=False
    )
```

profile of v0, /device:TPU:0, one launch (start us, length us, event | category | flops | bytes accessed | tf_op | source)
XLA Modules:
  0.0 121.3 jit_solution(946812768014044533)
XLA Ops:
  7.2 1.1 convert_reduce_fusion
  8.3 1.2 fusion.21
  9.5 1.6 %fusion.72 = (bf16[1,128,512]{2,1,0:T(8,128)(2,1)}, bf16[1,128,512]{2,1,0:T(8,128)(2,1)S(1)}) fusion(bf16[2,128,512]{2,1,0:T(8,128)(2,1)} %param.9), kind=kLoop, calls=%fused_computation.108 | loop fusion | bytes 524288 | tf_op jit(solution)/shard_map/slice | solution.py:41
  11.8 0.9 fusion.38
  12.7 1.2 %copy.84 = bf16[128,12,48]{2,1,0:T(8,128)(2,1)} copy(bf16[128,12,48]{0,2,1:T(8,128)(2,1)S(1)} %get-tuple-element.8) | data formatting | bytes 294912 | tf_op jit(solution)/shard_map/convert_element_type | solution.py:43
  14.0 24.4 %all-gather.3.cloned.1.call-done = bf16[128,96,48]{0,2,1:T(8,128)(2,1)} async-done(((bf16[128,12,48]{0,2,1:T(8,128)(2,1)}), bf16[128,96,48]{0,2,1:T(8,128)(2,1)}) %all-gather.3.cloned.1.call-update) | async-done | bytes 1179664 | tf_op jit(solution)/shard_map/all_gather | solution.py:58
  38.3 5.3 %copy.85 = bf16[128,96,48]{2,1,0:T(8,128)(2,1)S(1)} copy(bf16[128,96,48]{0,2,1:T(8,128)(2,1)} %all-gather.3.cloned.1.call-done) | data formatting | bytes 2359296 | tf_op jit(solution)/shard_map/all_gather | solution.py:58
  43.6 3.7 %fusion.76 = f32[128,12,96]{2,1,0:T(8,128)} fusion(bf16[128,12,48]{2,1,0:T(8,128)(2,1)} %copy.84, bf16[128,96,48]{2,1,0:T(8,128)(2,1)S(1)} %copy.85), kind=kOutput, calls=%fused_computation.112 | convolution fusion | flops 14155776 | bytes 1916928 | tf_op jit(solution)/shard_map/hik,hjk->hij/dot_general | solution.py:15
  47.4 2.7 %copy.86 = f32[128,12,96]{0,1,2:T(8,128)} copy(f32[128,12,96]{2,1,0:T(8,128)} %fusion.76) | data formatting | bytes 1179648 | tf_op jit(solution)/shard_map/hik,hjk->hij/dot_general | solution.py:15
  50.7 16.7 %reduce-scatter.2.cloned.1.call-done = f32[128,12,48]{0,1,2:T(8,128)} async-done(((f32[128,12,96]{0,1,2:T(8,128)}), f32[128,12,48]{0,1,2:T(8,128)}) %reduce-scatter.2.cloned.1.call-update) | async-done | bytes 294928 | tf_op jit(solution)/shard_map/reduce_scatter | solution.py:59
  67.5 1.2 %reduce_sum.92 = f32[12,48]{0,1:T(8,128)S(1)} reduce(f32[128,12,48]{0,1,2:T(8,128)} %reduce-scatter.2.cloned.1.call-done, f32[]{:T(128)} %constant.32.clone.1), dimensions={0}, to_apply=%region_3.0 | reduce | flops 73152 | bytes 297220 | tf_op jit(solution)/shard_map/reduce_sum | solution.py:8
  68.9 1.3 %multiply_reduce_fusion.1 = f32[12,48]{0,1:T(8,128)S(1)} fusion(f32[128,12,48]{0,1,2:T(8,128)} %reduce-scatter.2.cloned.1.call-done, f32[12,48]{0,1:T(8,128)S(1)} %copy.88), kind=kLoop, calls=%fused_computation.31 | loop fusion | flops 220608 | bytes 299520 | tf_op jit(solution)/shard_map/reduce_sum | solution.py:10
  71.7 0.9 fusion.24
  72.6 6.1 %all_gather.10 = bf16[128,12,96]{0,2,1:T(8,128)(2,1)S(1)} all-gather(bf16[128,12,48]{0,2,1:T(8,128)(2,1)S(1)} %get-tuple-element.6), channel_id=1, replica_groups=mesh['grp'=2,'row'=8,'col'=2] {'col'}, dimensions={2}, use_global_device_ids=true | all-gather | bytes 442368 | tf_op jit(solution)/shard_map/all_gather | solution.py:62
  78.6 0.9 copy.95
  79.5 4.6 %all-to-all-start = ((bf16[128,12,96]{0,1,2:T(8,128)(2,1)}), bf16[128,12,96]{0,1,2:T(8,128)(2,1)S(1)}, u32[]{:S(2)}, u32[]{:S(2)}) async-start(bf16[128,12,96]{0,1,2:T(8,128)(2,1)} %copy.95), calls=%async_computation.1 | async-start | bytes 786432 | tf_op jit(solution)/shard_map/all_to_all | solution.py:63
  84.1 1.1 fusion.8
  85.2 17.1 %all-to-all-done = bf16[128,12,96]{0,1,2:T(8,128)(2,1)S(1)} async-done(((bf16[128,12,96]{0,1,2:T(8,128)(2,1)}), bf16[128,12,96]{0,1,2:T(8,128)(2,1)S(1)}, u32[]{:S(2)}, u32[]{:S(2)}) %all-to-all-start) | async-done | bytes 294944 | tf_op jit(solution)/shard_map/all_to_all | solution.py:63
  102.4 1.2 %copy.98 = bf16[128,96,12]{1,2,0:T(8,128)(2,1)} copy(bf16[128,96,12]{0,1,2:T(8,128)(2,1)S(1)} %all_to_all.16) | data formatting | bytes 589824 | tf_op jit(solution)/shard_map/all_to_all | solution.py:63
  103.7 5.3 %copy.99 = bf16[128,96,48]{2,1,0:T(8,128)(2,1)S(1)} copy(bf16[128,96,48]{0,2,1:T(8,128)(2,1)} %all-gather.5.cloned.1.call-done) | data formatting | bytes 2359296 | tf_op jit(solution)/shard_map/all_gather | solution.py:65
  109.0 2.0 %fusion.74 = (f32[12,48]{1,0:T(8,128)S(1)}, f32[128,12,48]{2,1,0:T(8,128)S(1)}) fusion(bf16[128,96,12]{1,2,0:T(8,128)(2,1)} %copy.98, bf16[128,96,48]{2,1,0:T(8,128)(2,1)S(1)} %copy.99), kind=kOutput, calls=%fused_computation.110 | convolution fusion | flops 14228928 | bytes 1771776 | tf_op jit(solution)/shard_map/hki,hkj->hij/dot_general | solution.py:19
  111.3 0.6 copy-done.2
  112.7 0.5 fusion.53
  113.6 1.1 fusion.14
  (73 shorter events, 4.4 us)
Async XLA Ops:
  6.5 106.2 %copy-start = (bf16[128,1024]{1,0:T(8,128)(2,1)S(1)}, bf16[128,1024]{1,0:T(8,128)(2,1)}, u32[]{:S(2)}) copy-start(bf16[128,1024]{1,0:T(8,128)(2,1)} %param.12) | copy-start | bytes 786436
  6.5 4.9 %copy-start.4 = (bf16[12,48,128]{2,1,0:T(8,128)(2,1)S(1)}, bf16[12,48,128]{2,1,0:T(8,128)(2,1)}, u32[]{:S(2)}) copy-start(bf16[12,48,128]{2,1,0:T(8,128)(2,1)} %param.7) | copy-start | bytes 442372
  6.5 31.8 %all-gather.3.cloned.1.call-start = ((), (), s32[]{:S(2)}) async-start(), calls=%async_computation.2 | async-start | bytes 1327104 | tf_op jit(solution)/shard_map/all_gather | solution.py:58
  8.3 3.5 %copy-start.10 = (f32[12,48]{1,0:T(8,128)}, f32[12,48]{1,0:T(8,128)S(1)}, u32[]{:S(2)}) copy-start(f32[12,48]{1,0:T(8,128)S(1)} %broadcast_multiply_fusion.4) | copy-start | bytes 6916
  9.5 3.1 %copy-start.14 = (f32[12,48]{1,0:T(8,128)}, f32[12,48]{1,0:T(8,128)S(1)}, u32[]{:S(2)}) copy-start(f32[12,48]{1,0:T(8,128)S(1)} %add_rsqrt_fusion.4) | copy-start | bytes 6916
  11.4 1.2 %copy-start.7 = (f32[12,48]{1,0:T(8,128)}, f32[12,48]{1,0:T(8,128)S(1)}, u32[]{:S(2)}) copy-start(f32[12,48]{1,0:T(8,128)S(1)} %broadcast_multiply_fusion.5) | copy-start | bytes 6916
  12.7 54.8 %reduce-scatter.2.cloned.1.call-start = ((), (), s32[]{:S(2)}) async-start(), calls=%async_computation.3 | async-start | bytes 1179648 | tf_op jit(solution)/shard_map/reduce_scatter | solution.py:59
  47.4 2.8 %copy-start.5 = (bf16[1,128,512]{2,1,0:T(8,128)(2,1)S(1)}, bf16[1,128,512]{2,1,0:T(8,128)(2,1)}, u32[]{:S(2)}) copy-start(bf16[1,128,512]{2,1,0:T(8,128)(2,1)} %get-tuple-element.9) | copy-start | bytes 393220
  47.4 2.9 %copy-start.11 = (f32[12,48]{1,0:T(8,128)S(1)}, f32[12,48]{1,0:T(8,128)}, u32[]{:S(2)}) copy-start(f32[12,48]{1,0:T(8,128)} %copy-done.10) | copy-start | bytes 6916
  47.4 2.9 %copy-start.15 = (f32[12,48]{1,0:T(8,128)S(1)}, f32[12,48]{1,0:T(8,128)}, u32[]{:S(2)}) copy-start(f32[12,48]{1,0:T(8,128)} %copy-done.14) | copy-start | bytes 6916
  47.4 3.0 %copy-start.17 = (bf16[2,128,128]{2,1,0:T(8,128)(2,1)S(1)}, bf16[2,128,128]{2,1,0:T(8,128)(2,1)}, u32[]{:S(2)}) copy-start(bf16[2,128,128]{2,1,0:T(8,128)(2,1)} %param.10) | copy-start | bytes 196612
  50.2 53.5 %all-gather.5.cloned.1.call-start = ((), (), s32[]{:S(2)}) async-start(), calls=%async_computation.4 | async-start | bytes 1327104 | tf_op jit(solution)/shard_map/all_gather | solution.py:65
  50.7 19.9 %copy-start.8 = (f32[12,48]{1,0:T(8,128)S(1)}, f32[12,48]{1,0:T(8,128)}, u32[]{:S(2)}) copy-start(f32[12,48]{1,0:T(8,128)} %copy-done.7) | copy-start | bytes 6916
  50.7 19.9 %copy-start.12 = (bf16[2,128,128]{2,1,0:T(8,128)(2,1)S(1)}, bf16[2,128,128]{2,1,0:T(8,128)(2,1)}, u32[]{:S(2)}) copy-start(bf16[2,128,128]{2,1,0:T(8,128)(2,1)} %param.11) | copy-start | bytes 196612
  67.5 2.9 %copy-start.3 = (f32[128,12,48]{0,1,2:T(8,128)S(1)}, f32[128,12,48]{0,1,2:T(8,128)}, u32[]{:S(2)}) copy-start(f32[128,12,48]{0,1,2:T(8,128)} %reduce-scatter.2.cloned.1.call-done) | copy-start | bytes 884740
  71.0 13.1 %copy-start.1 = (f32[12,48,128]{2,1,0:T(8,128)}, f32[12,48,128]{2,1,0:T(8,128)S(1)}, u32[]{:S(2)}) copy-start(f32[12,48,128]{2,1,0:T(8,128)S(1)} %get-tuple-element.12) | copy-start | bytes 884740
  79.5 22.8 %all-to-all-start = ((bf16[128,12,96]{0,1,2:T(8,128)(2,1)}), bf16[128,12,96]{0,1,2:T(8,128)(2,1)S(1)}, u32[]{:S(2)}, u32[]{:S(2)}) async-start(bf16[128,12,96]{0,1,2:T(8,128)(2,1)} %copy.95), calls=%async_computation.1 | async-start | bytes 786432 | tf_op jit(solution)/shard_map/all_to_all | solution.py:63
  111.0 1.0 copy-start.2
  111.0 1.0 copy-start.6
  111.0 1.0 copy-start.9
  111.0 1.0 copy-start.13
  112.7 0.9 copy-start.16
Sparse Core Ops, SparseCore 0:
  12.8 25.4 all-gather.2
  50.3 17.1 reduce-scatter.1
  72.7 30.0 all-gather.4
where the time goes:
time: 122 us; the launch traced here: 121 us
  waiting for transfers between devices  58.2 us (48%)
  local copies, waits for them, and re-layouts  20.1 us (16%)
  between operations  14.2 us (12%)
  matrix products  10.2 us (8%)
  other arithmetic  7.78 us (6%)
  blocking collectives  6.08 us (5%)
  starting transfers between devices  4.69 us (4%)
    all_gather x2, waiting for transfers between devices, body(): lax.all_gather(right_side, 'row', axis=1, tiled=True)  24.4 us
    all_to_all x1, waiting for transfers between devices, body(): lax.all_to_all(left_rows, 'row', split_axis=2, concat_axis=1, tiled=True)  17.1 us
    reduce_scatter x1, waiting for transfers between devices, body(): lax.psum_scatter(partial_rows, 'col', scatter_dimension=2, tiled=True)  16.7 us
    all_gather x2, local copies, waits for them, and re-layouts, body(): lax.all_gather(right_side, 'row', axis=1, tiled=True)  10.6 us
    all_gather x1, blocking collectives, body(): left_rows = lax.all_gather(left_side, 'col', axis=2, tiled=True)  6.08 us
    all_to_all x1, starting transfers between devices, body(): lax.all_to_all(left_rows, 'row', split_axis=2, concat_axis=1, tiled=True)  4.6 us
    dot_general x1, matrix products, contract_rows(): jnp.einsum('hik,hjk->hij', left_side, right_side, preferred_element_type=...  3.75 us
    reduce_sum x5, other arithmetic, layer_norm(): spread = jnp.mean(centred * centred, axis=along, keepdims=True)  3.23 us
  transfers between devices with their start and end apart: 4, of which 3 were waited for; matrix products, arithmetic and copies ran while one was open for 4% of the time, Pallas kernels for 0%

commit v1 on v0

--- a/solution.py
+++ b/solution.py
@@ -2,6 +2,18 @@
 import jax.numpy as jnp
 from jax import lax
 from jax.sharding import PartitionSpec as P
+
+
+def exchange_directly(shard, axis, split, join):
+    ways, here = (lax.axis_size(axis), lax.axis_index(axis))
+    width = shard.shape[split] // ways
+    turned = jnp.roll(shard, -here * width, axis=split)
+    got = [lax.slice_in_dim(turned, 0, width, axis=split)]
+    for far in range(1, ways):
+        sent = lax.slice_in_dim(turned, far * width, (far + 1) * width, axis=split)
+        got.append(lax.ppermute(sent, axis, [(d, (d + far) % ways) for d in range(ways)]))
+    line = jnp.concatenate(got[::-1], axis=join)
+    return jnp.roll(line, (here + 1) * got[0].shape[join], axis=join)
 
 
 def layer_norm(values, along):
@@ -60,7 +72,7 @@
     stream = finish(pair, mixed_sum, gate_value, 0)
     left_side, right_side, gate_value = project(stream, 1)
     left_rows = lax.all_gather(left_side, "col", axis=2, tiled=True)
-    column_strip = lax.all_to_all(left_rows, "row", split_axis=2, concat_axis=1, tiled=True)
+    column_strip = exchange_directly(left_rows, "row", 2, 1)
     mixed_sum = contract_columns(
         column_strip, lax.all_gather(right_side, "row", axis=1, tiled=True)
     )

time: 122 us -> 127 us (1.041)
  starting transfers between devices: 4.69 us -> 7.45 us
  waiting for transfers between devices: 58.2 us -> 60.5 us
    all_to_all x1 -> x0, waiting for transfers between devices: 17.1 us -> none  [body(): lax.all_to_all(left_rows, 'row', split_axis=2, concat_axis=1, tiled=True)]
    all_gather x2, waiting for transfers between devices: 24.4 us -> 37.8 us  [body(): lax.all_gather(right_side, 'row', axis=1, tiled=True)]
    ppermute x0 -> x7, starting transfers between devices: none -> 7.36 us  [exchange_directly(): lax.ppermute(sent, axis, [(d, (d + far) % ways) for d in range(ways)])]
    ppermute x0 -> x7, waiting for transfers between devices: none -> 5.92 us  [exchange_directly(): lax.ppermute(sent, axis, [(d, (d + far) % ways) for d in range(ways)])]
    all_to_all x1 -> x0, starting transfers between devices: 4.6 us -> none  [body(): lax.all_to_all(left_rows, 'row', split_axis=2, concat_axis=1, tiled=True)]
    dynamic_slice x0 -> x2, local copies, waits for them, and re-layouts: none -> 1.45 us  [exchange_directly(): return jnp.roll(line, (here + 1) * got[0].shape[join], axis=join)]
    all_to_all x3 -> x0, local copies, waits for them, and re-layouts: 1.33 us -> none  [body(): lax.all_to_all(left_rows, 'row', split_axis=2, concat_axis=1, tiled=True)]
  transfers between devices with their start and end apart: 4 -> 10, of which waited for: 3 -> 4; matrix products, arithmetic and copies ran while one was open for 4% -> 3% of each run, Pallas kernels for 0% -> 0%
where the time goes in v1:
time: 127 us; the launch traced here: 126 us
  waiting for transfers between devices  60.5 us (48%)
  local copies, waits for them, and re-layouts  19.6 us (15%)
  between operations  14.3 us (11%)
  matrix products  10.2 us (8%)
  other arithmetic  7.99 us (6%)
  starting transfers between devices  7.45 us (6%)
  blocking collectives  6.07 us (5%)
    all_gather x2, waiting for transfers between devices, body(): lax.all_gather(right_side, 'row', axis=1, tiled=True)  37.8 us
    reduce_scatter x1, waiting for transfers between devices, body(): lax.psum_scatter(partial_rows, 'col', scatter_dimension=2, tiled=True)  16.7 us
    all_gather x2, local copies, waits for them, and re-layouts, body(): lax.all_gather(right_side, 'row', axis=1, tiled=True)  10.6 us
    ppermute x7, starting transfers between devices, exchange_directly(): lax.ppermute(sent, axis, [(d, (d + far) % ways) for d in range(ways)])  7.36 us
    all_gather x1, blocking collectives, body(): left_rows = lax.all_gather(left_side, 'col', axis=2, tiled=True)  6.07 us
    ppermute x7, waiting for transfers between devices, exchange_directly(): lax.ppermute(sent, axis, [(d, (d + far) % ways) for d in range(ways)])  5.92 us
    dot_general x1, matrix products, contract_rows(): jnp.einsum('hik,hjk->hij', left_side, right_side, preferred_element_type=...  3.74 us
    reduce_sum x5, other arithmetic, layer_norm(): spread = jnp.mean(centred * centred, axis=along, keepdims=True)  3.23 us
  transfers between devices with their start and end apart: 10, of which 4 were waited for; matrix products, arithmetic and copies ran while one was open for 3% of the time, Pallas kernels for 0%

profile of v1, /device:TPU:0, one launch (start us, length us, event | category | flops | bytes accessed | tf_op | source)
XLA Modules:
  0.0 126.1 jit_solution(12656868659926911051)
XLA Ops:
  7.2 1.1 convert_reduce_fusion
  8.3 1.2 fusion.21
  9.5 1.6 %fusion.74 = (bf16[1,128,512]{2,1,0:T(8,128)(2,1)}, bf16[1,128,512]{2,1,0:T(8,128)(2,1)S(1)}) fusion(bf16[2,128,512]{2,1,0:T(8,128)(2,1)} %param.9), kind=kLoop, calls=%fused_computation.129 | loop fusion | bytes 524288 | tf_op jit(solution)/shard_map/slice | solution.py:53
  11.8 0.9 fusion.39
  12.7 1.2 copy.77
  14.0 24.4 %all-gather.3.cloned.1.call-done = bf16[128,96,48]{0,2,1:T(8,128)(2,1)} async-done(((bf16[128,12,48]{0,2,1:T(8,128)(2,1)}), bf16[128,96,48]{0,2,1:T(8,128)(2,1)}) %all-gather.3.cloned.1.call-update) | async-done | bytes 1179664 | tf_op jit(solution)/shard_map/all_gather | solution.py:70
  38.4 5.3 %copy.78 = bf16[128,96,48]{2,1,0:T(8,128)(2,1)S(1)} copy(bf16[128,96,48]{0,2,1:T(8,128)(2,1)} %all-gather.3.cloned.1.call-done) | data formatting | bytes 2359296 | tf_op jit(solution)/shard_map/all_gather | solution.py:70
  43.7 3.7 %fusion.78 = f32[128,12,96]{2,1,0:T(8,128)} fusion(bf16[128,12,48]{2,1,0:T(8,128)(2,1)} %copy.77, bf16[128,96,48]{2,1,0:T(8,128)(2,1)S(1)} %copy.78), kind=kOutput, calls=%fused_computation.133 | convolution fusion | flops 14155776 | bytes 1916928 | tf_op jit(solution)/shard_map/hik,hjk->hij/dot_general | solution.py:27
  47.4 2.7 %copy.79 = f32[128,12,96]{0,1,2:T(8,128)} copy(f32[128,12,96]{2,1,0:T(8,128)} %fusion.78) | data formatting | bytes 1179648 | tf_op jit(solution)/shard_map/hik,hjk->hij/dot_general | solution.py:27
  50.8 16.7 %reduce-scatter.2.cloned.1.call-done = f32[128,12,48]{0,1,2:T(8,128)} async-done(((f32[128,12,96]{0,1,2:T(8,128)}), f32[128,12,48]{0,1,2:T(8,128)}) %reduce-scatter.2.cloned.1.call-update) | async-done | bytes 294928 | tf_op jit(solution)/shard_map/reduce_scatter | solution.py:71
  67.5 1.2 reduce_sum.92
  68.9 1.3 %multiply_reduce_fusion.1 = f32[12,48]{0,1:T(8,128)S(1)} fusion(f32[128,12,48]{0,1,2:T(8,128)} %reduce-scatter.2.cloned.1.call-done, f32[12,48]{0,1:T(8,128)S(1)} %copy.81), kind=kLoop, calls=%fused_computation.33 | loop fusion | flops 220608 | bytes 299520 | tf_op jit(solution)/shard_map/reduce_sum | solution.py:22
  71.7 0.9 fusion.25
  72.5 6.1 %all_gather.10 = bf16[128,12,96]{0,2,1:T(8,128)(2,1)S(1)} all-gather(bf16[128,12,48]{0,2,1:T(8,128)(2,1)S(1)} %get-tuple-element.6), channel_id=1, replica_groups=mesh['grp'=2,'row'=8,'col'=2] {'col'}, dimensions={2}, use_global_device_ids=true | all-gather | bytes 442368 | tf_op jit(solution)/shard_map/all_gather | solution.py:74
  78.9 1.8 %collective-permute-start = (bf16[128,12,12]{0,2,1:T(8,128)(2,1)S(1)}, bf16[128,12,12]{0,2,1:T(8,128)(2,1)S(1)}, u32[]{:S(2)}, u32[]{:S(2)}) collective-permute-start(bf16[128,12,12]{0,2,1:T(8,128)(2,1)S(1)} %get-tuple-element.15), channel_id=1, source_target_pairs={{0,14},{2,0},{4,2},{6,4},{8,6},{10,8},{12,10},{14,12},{1,15},{3,1}... | collective-permute-start | bytes 110600 | tf_op jit(solution)/shard_map/ppermute | solution.py:14
  80.7 1.1 fusion.8
  81.8 1.6 %collective-permute-start.1 = (bf16[128,12,12]{0,2,1:T(8,128)(2,1)S(1)}, bf16[128,12,12]{0,2,1:T(8,128)(2,1)S(1)}, u32[]{:S(2)}, u32[]{:S(2)}) collective-permute-start(bf16[128,12,12]{0,2,1:T(8,128)(2,1)S(1)} %get-tuple-element.14), channel_id=1, source_target_pairs={{0,12},{2,14},{4,0},{6,2},{8,4},{10,6},{12,8},{14,10},{1,13},{3,15... | collective-permute-start | bytes 110600 | tf_op jit(solution)/shard_map/ppermute | solution.py:14
  83.4 2.7 %collective-permute-start.3 = (bf16[128,12,12]{0,2,1:T(8,128)(2,1)S(1)}, bf16[128,12,12]{0,2,1:T(8,128)(2,1)S(1)}, u32[]{:S(2)}, u32[]{:S(2)}) collective-permute-start(bf16[128,12,12]{0,2,1:T(8,128)(2,1)S(1)} %get-tuple-element.12), channel_id=1, source_target_pairs={{0,8},{2,10},{4,12},{6,14},{8,0},{10,2},{12,4},{14,6},{1,9},{3,11}... | collective-permute-start | bytes 110600 | tf_op jit(solution)/shard_map/ppermute | solution.py:14
  87.4 5.9 %collective-permute-done.3 = bf16[128,12,12]{0,2,1:T(8,128)(2,1)S(1)} collective-permute-done((bf16[128,12,12]{0,2,1:T(8,128)(2,1)S(1)}, bf16[128,12,12]{0,2,1:T(8,128)(2,1)S(1)}, u32[]{:S(2)}, u32[]{:S(2)}) %collective-permute-start.3) | collective-permute-done | bytes 36896 | tf_op jit(solution)/shard_map/ppermute | solution.py:14
  93.6 1.4 %copy.88 = bf16[128,96,12]{1,2,0:T(8,128)(2,1)} copy(bf16[128,96,12]{0,2,1:T(8,128)(2,1)S(1)} %constant_dynamic-slice_fusion) | data formatting | bytes 589824 | tf_op jit(solution)/shard_map/jit(_roll_dynamic)/dynamic_slice | solution.py:16
  95.1 13.4 %all-gather.5.cloned.1.call-done = bf16[128,96,48]{0,2,1:T(8,128)(2,1)} async-done(((bf16[128,12,48]{0,2,1:T(8,128)(2,1)}), bf16[128,96,48]{0,2,1:T(8,128)(2,1)}) %all-gather.5.cloned.1.call-update) | async-done | bytes 1179664 | tf_op jit(solution)/shard_map/all_gather | solution.py:77
  108.5 5.3 %copy.89 = bf16[128,96,48]{2,1,0:T(8,128)(2,1)S(1)} copy(bf16[128,96,48]{0,2,1:T(8,128)(2,1)} %all-gather.5.cloned.1.call-done) | data formatting | bytes 2359296 | tf_op jit(solution)/shard_map/all_gather | solution.py:77
  113.8 2.0 %fusion.76 = (f32[12,48]{1,0:T(8,128)S(1)}, f32[128,12,48]{2,1,0:T(8,128)S(1)}) fusion(bf16[128,96,12]{1,2,0:T(8,128)(2,1)} %copy.88, bf16[128,96,48]{2,1,0:T(8,128)(2,1)S(1)} %copy.89), kind=kOutput, calls=%fused_computation.131 | convolution fusion | flops 14228928 | bytes 1771776 | tf_op jit(solution)/shard_map/hki,hkj->hij/dot_general | solution.py:31
  118.5 1.1 fusion.14
  (101 shorter events, 7.2 us)
Async XLA Ops:
  6.5 111.0 %copy-start = (bf16[128,1024]{1,0:T(8,128)(2,1)S(1)}, bf16[128,1024]{1,0:T(8,128)(2,1)}, u32[]{:S(2)}) copy-start(bf16[128,1024]{1,0:T(8,128)(2,1)} %param.12) | copy-start | bytes 786436
  6.5 4.9 %copy-start.4 = (bf16[12,48,128]{2,1,0:T(8,128)(2,1)S(1)}, bf16[12,48,128]{2,1,0:T(8,128)(2,1)}, u32[]{:S(2)}) copy-start(bf16[12,48,128]{2,1,0:T(8,128)(2,1)} %param.7) | copy-start | bytes 442372
  6.5 31.8 %all-gather.3.cloned.1.call-start = ((), (), s32[]{:S(2)}) async-start(), calls=%async_computation.1 | async-start | bytes 1327104 | tf_op jit(solution)/shard_map/all_gather | solution.py:70
  8.3 3.5 %copy-start.10 = (f32[12,48]{1,0:T(8,128)}, f32[12,48]{1,0:T(8,128)S(1)}, u32[]{:S(2)}) copy-start(f32[12,48]{1,0:T(8,128)S(1)} %broadcast_multiply_fusion.4) | copy-start | bytes 6916
  9.5 3.1 %copy-start.14 = (f32[12,48]{1,0:T(8,128)}, f32[12,48]{1,0:T(8,128)S(1)}, u32[]{:S(2)}) copy-start(f32[12,48]{1,0:T(8,128)S(1)} %add_rsqrt_fusion.4) | copy-start | bytes 6916
  11.4 1.2 copy-start.7
  12.7 54.8 %reduce-scatter.2.cloned.1.call-start = ((), (), s32[]{:S(2)}) async-start(), calls=%async_computation.2 | async-start | bytes 1179648 | tf_op jit(solution)/shard_map/reduce_scatter | solution.py:71
  47.4 2.8 %copy-start.5 = (bf16[1,128,512]{2,1,0:T(8,128)(2,1)S(1)}, bf16[1,128,512]{2,1,0:T(8,128)(2,1)}, u32[]{:S(2)}) copy-start(bf16[1,128,512]{2,1,0:T(8,128)(2,1)} %get-tuple-element.16) | copy-start | bytes 393220
  47.4 3.0 %copy-start.11 = (f32[12,48]{1,0:T(8,128)S(1)}, f32[12,48]{1,0:T(8,128)}, u32[]{:S(2)}) copy-start(f32[12,48]{1,0:T(8,128)} %copy-done.10) | copy-start | bytes 6916
  47.4 3.0 %copy-start.15 = (f32[12,48]{1,0:T(8,128)S(1)}, f32[12,48]{1,0:T(8,128)}, u32[]{:S(2)}) copy-start(f32[12,48]{1,0:T(8,128)} %copy-done.14) | copy-start | bytes 6916
  47.4 3.0 %copy-start.17 = (bf16[2,128,128]{2,1,0:T(8,128)(2,1)S(1)}, bf16[2,128,128]{2,1,0:T(8,128)(2,1)}, u32[]{:S(2)}) copy-start(bf16[2,128,128]{2,1,0:T(8,128)(2,1)} %param.10) | copy-start | bytes 196612
  50.2 58.3 %all-gather.5.cloned.1.call-start = ((), (), s32[]{:S(2)}) async-start(), calls=%async_computation.3 | async-start | bytes 1327104 | tf_op jit(solution)/shard_map/all_gather | solution.py:77
  50.8 19.9 %copy-start.8 = (f32[12,48]{1,0:T(8,128)S(1)}, f32[12,48]{1,0:T(8,128)}, u32[]{:S(2)}) copy-start(f32[12,48]{1,0:T(8,128)} %copy-done.7) | copy-start | bytes 6916
  50.8 19.9 %copy-start.12 = (bf16[2,128,128]{2,1,0:T(8,128)(2,1)S(1)}, bf16[2,128,128]{2,1,0:T(8,128)(2,1)}, u32[]{:S(2)}) copy-start(bf16[2,128,128]{2,1,0:T(8,128)(2,1)} %param.11) | copy-start | bytes 196612
  67.5 2.9 %copy-start.3 = (f32[128,12,48]{0,1,2:T(8,128)S(1)}, f32[128,12,48]{0,1,2:T(8,128)}, u32[]{:S(2)}) copy-start(f32[128,12,48]{0,1,2:T(8,128)} %reduce-scatter.2.cloned.1.call-done) | copy-start | bytes 884740
  71.0 9.7 %copy-start.1 = (f32[12,48,128]{2,1,0:T(8,128)}, f32[12,48,128]{2,1,0:T(8,128)S(1)}, u32[]{:S(2)}) copy-start(f32[12,48,128]{2,1,0:T(8,128)S(1)} %get-tuple-element.19) | copy-start | bytes 884740
  78.9 7.3 %collective-permute-start = (bf16[128,12,12]{0,2,1:T(8,128)(2,1)S(1)}, bf16[128,12,12]{0,2,1:T(8,128)(2,1)S(1)}, u32[]{:S(2)}, u32[]{:S(2)}) collective-permute-start(bf16[128,12,12]{0,2,1:T(8,128)(2,1)S(1)} %get-tuple-element.15), channel_id=1, source_target_pairs={{0,14},{2,0},{4,2},{6,4},{8,6},{10,8},{12,10},{14,12},{1,15},{3,1}... | collective-permute-start | bytes 110600 | tf_op jit(solution)/shard_map/ppermute | solution.py:14
  81.8 5.2 %collective-permute-start.1 = (bf16[128,12,12]{0,2,1:T(8,128)(2,1)S(1)}, bf16[128,12,12]{0,2,1:T(8,128)(2,1)S(1)}, u32[]{:S(2)}, u32[]{:S(2)}) collective-permute-start(bf16[128,12,12]{0,2,1:T(8,128)(2,1)S(1)} %get-tuple-element.14), channel_id=1, source_target_pairs={{0,12},{2,14},{4,0},{6,2},{8,4},{10,6},{12,8},{14,10},{1,13},{3,15... | collective-permute-start | bytes 110600 | tf_op jit(solution)/shard_map/ppermute | solution.py:14
  83.4 4.0 %collective-permute-start.2 = (bf16[128,12,12]{0,2,1:T(8,128)(2,1)S(1)}, bf16[128,12,12]{0,2,1:T(8,128)(2,1)S(1)}, u32[]{:S(2)}, u32[]{:S(2)}) collective-permute-start(bf16[128,12,12]{0,2,1:T(8,128)(2,1)S(1)} %get-tuple-element.13), channel_id=1, source_target_pairs={{0,10},{2,12},{4,14},{6,0},{8,2},{10,4},{12,6},{14,8},{1,11},{3,13... | collective-permute-start | bytes 110600 | tf_op jit(solution)/shard_map/ppermute | solution.py:14
  83.4 9.9 %collective-permute-start.3 = (bf16[128,12,12]{0,2,1:T(8,128)(2,1)S(1)}, bf16[128,12,12]{0,2,1:T(8,128)(2,1)S(1)}, u32[]{:S(2)}, u32[]{:S(2)}) collective-permute-start(bf16[128,12,12]{0,2,1:T(8,128)(2,1)S(1)} %get-tuple-element.12), channel_id=1, source_target_pairs={{0,8},{2,10},{4,12},{6,14},{8,0},{10,2},{12,4},{14,6},{1,9},{3,11}... | collective-permute-start | bytes 110600 | tf_op jit(solution)/shard_map/ppermute | solution.py:14
  86.1 7.2 %collective-permute-start.4 = (bf16[128,12,12]{0,2,1:T(8,128)(2,1)S(1)}, bf16[128,12,12]{0,2,1:T(8,128)(2,1)S(1)}, u32[]{:S(2)}, u32[]{:S(2)}) collective-permute-start(bf16[128,12,12]{0,2,1:T(8,128)(2,1)S(1)} %get-tuple-element.11), channel_id=1, source_target_pairs={{0,6},{2,8},{4,10},{6,12},{8,14},{10,0},{12,2},{14,4},{1,7},{3,9},... | collective-permute-start | bytes 110600 | tf_op jit(solution)/shard_map/ppermute | solution.py:14
  86.2 7.2 %collective-permute-start.5 = (bf16[128,12,12]{0,2,1:T(8,128)(2,1)S(1)}, bf16[128,12,12]{0,2,1:T(8,128)(2,1)S(1)}, u32[]{:S(2)}, u32[]{:S(2)}) collective-permute-start(bf16[128,12,12]{0,2,1:T(8,128)(2,1)S(1)} %get-tuple-element.10), channel_id=1, source_target_pairs={{0,4},{2,6},{4,8},{6,10},{8,12},{10,14},{12,0},{14,2},{1,5},{3,7},... | collective-permute-start | bytes 110600 | tf_op jit(solution)/shard_map/ppermute | solution.py:14
  87.0 6.4 %collective-permute-start.6 = (bf16[128,12,12]{0,2,1:T(8,128)(2,1)S(1)}, bf16[128,12,12]{0,2,1:T(8,128)(2,1)S(1)}, u32[]{:S(2)}, u32[]{:S(2)}) collective-permute-start(bf16[128,12,12]{0,2,1:T(8,128)(2,1)S(1)} %get-tuple-element.9), channel_id=1, source_target_pairs={{0,2},{2,4},{4,6},{6,8},{8,10},{10,12},{12,14},{14,0},{1,3},{3,5},... | collective-permute-start | bytes 110600 | tf_op jit(solution)/shard_map/ppermute | solution.py:14
  115.8 1.0 copy-start.6
  (4 other events, 3.9 us)
Sparse Core Ops, SparseCore 0:
  12.8 25.4 all-gather.2
  50.3 17.1 reduce-scatter.1
  86.3 22.1 all-gather.4
